TPU v7x, 32 devices: a whole 2x2x4 slice. The times are simulated.
32 devices in a mesh: rep: 4 (over y, x), fsdp: 4 (over z), ctx: 2 (over core).
Axes of the slice: x: 2, y: 2, z: 4, core: 2. Of those that a mesh axis runs over, the one named last changes fastest.
Arguments:
- inputs: bfloat16 [2, 16, 1024, 768], P(None, ('rep', 'fsdp'), 'ctx'), may hold values from -6 to 6
- weight_qkv: bfloat16 [768, 2304], P('fsdp'), may hold values from -0.21875 to 0.21875
- bias_query: bfloat16 [768], P('fsdp'), may hold values from -3 to 3
- bias_value: bfloat16 [768], P('fsdp'), may hold values from -3 to 3
- weight_mix: bfloat16 [768, 768], P('fsdp'), may hold values from -1.75 to 1.75
- bias_mix: bfloat16 [768], P('fsdp'), may hold values from -2 to 2
- gain_attn: bfloat16 [768], P('fsdp'), may hold values from 0.099609375 to 1.8984375
- shift_attn: bfloat16 [768], P('fsdp'), may hold values from -2 to 2
- gain_mlp: bfloat16 [768], P('fsdp'), may hold values from 0.099609375 to 1.8984375
- shift_mlp: bfloat16 [768], P('fsdp'), may hold values from -2 to 2
- weight_up: bfloat16 [768, 3072], P('fsdp'), may hold values from -0.21875 to 0.21875
- bias_up: bfloat16 [3072], P('fsdp'), may hold values from -3 to 3
- weight_down: bfloat16 [3072, 768], P('fsdp'), may hold values from -0.109375 to 0.109375
- bias_down: bfloat16 [768], P('fsdp'), may hold values from -2 to 2
- cotangent: bfloat16 [2, 16, 1024, 768], P(None, ('rep', 'fsdp'), 'ctx'), may hold values from -6 to 6
Outputs:
- outputs: bfloat16 [2, 16, 1024, 768], P(None, ('rep', 'fsdp'), 'ctx')
- grad_inputs: float32 [2, 16, 1024, 768], P(None, ('rep', 'fsdp'), 'ctx')
- weight_qkv_grad: float32 [768, 2304], P('fsdp')
- bias_query_grad: float32 [768], P('fsdp')
- bias_value_grad: float32 [768], P('fsdp')
- weight_mix_grad: float32 [768, 768], P('fsdp')
- bias_mix_grad: float32 [768], P('fsdp')
- gain_attn_grad: float32 [768], P('fsdp')
- shift_attn_grad: float32 [768], P('fsdp')
- gain_mlp_grad: float32 [768], P('fsdp')
- shift_mlp_grad: float32 [768], P('fsdp')
- weight_up_grad: float32 [768, 3072], P('fsdp')
- bias_up_grad: float32 [3072], P('fsdp')
- weight_down_grad: float32 [3072, 768], P('fsdp')
- bias_down_grad: float32 [768], P('fsdp')
All inputs are finite; a program needn't handle non-finite values.
Results may differ from a plain program's by a relative error of at most 0.018.
Values may be sent and summed in bfloat16 or wider, within the bound.
A program may use at most 320 MiB of HBM per device.

v0:
```python
from functools import partial
import jax
import jax.numpy as jnp
from jax import lax
from jax.sharding import PartitionSpec as P

H = 12
EPS = 1e-05


def from_behind(x, axis, by):
    peers = lax.axis_size(axis)
    pairs = [(i, i + by) for i in range(peers) if 0 <= i + by < peers]
    return lax.ppermute(x, axis, pairs)


def for_sending(x):

    def short(part):
        return part.astype(jnp.bfloat16) if part.dtype == jnp.float32 else part

    return jax.tree.map(short, x)


def norm_stats(values):
    center = values - jnp.mean(values, axis=-1, keepdims=True)
    inverse = lax.rsqrt(jnp.mean(center * center, axis=-1, keepdims=True) + EPS)
    return (center * inverse, inverse)


def norm_back(grad_norm, normal, inverse, gain):
    scaled = grad_norm * gain
    return inverse * (
        scaled
        - jnp.mean(scaled, axis=-1, keepdims=True)
        - normal * jnp.mean(scaled * normal, axis=-1, keepdims=True)
    )


def column_sum(values):
    return jnp.sum(values.astype(jnp.float32), axis=(0, 1))


def outer_sum(left, right):
    return jnp.einsum("sri,srj->ij", left, right, preferred_element_type=jnp.float32)


def project(left, weight):
    return jnp.einsum("sri,ij->srj", left, weight, preferred_element_type=jnp.float32)


def project_back(grad_rows, weight):
    return jnp.einsum("srj,ij->sri", grad_rows, weight, preferred_element_type=jnp.float32)


def split_heads(values):
    return values.reshape(values.shape[0], values.shape[1], H, values.shape[2] // H)


def attention_scores(query_heads, key_heads, allowed, factor):
    raw = jnp.einsum("sqhd,skhd->shqk", query_heads, key_heads, preferred_element_type=jnp.float32)
    return jnp.where(allowed, raw * factor, -1e30)


def local(
    inputs,
    weight_qkv,
    bias_query,
    bias_value,
    weight_mix,
    bias_mix,
    gain_attn,
    shift_attn,
    gain_mlp,
    shift_mlp,
    weight_up,
    bias_up,
    weight_down,
    bias_down,
    cotangent,
):
    shards = (
        weight_qkv,
        bias_query,
        bias_value,
        weight_mix,
        bias_mix,
        gain_attn,
        shift_attn,
        gain_mlp,
        shift_mlp,
        weight_up,
        bias_up,
        weight_down,
        bias_down,
    )
    width = weight_qkv.shape[1] // 3
    factor = (width // H) ** (-0.5)
    rows = inputs.shape[2]
    owners = lax.axis_size("fsdp")
    ctx_index = lax.axis_index("ctx")
    query_pos = lax.broadcasted_iota(jnp.int32, (rows, 2 * rows), 0)
    key_pos = lax.broadcasted_iota(jnp.int32, (rows, 2 * rows), 1) - rows
    allowed = (key_pos <= query_pos) & ((key_pos >= 0) | (ctx_index > 0))
    whole_zeros = tuple(
        (jnp.zeros((item.shape[0] * owners,) + item.shape[1:], jnp.float32) for item in shards)
    )
    bf16 = jnp.bfloat16
    f32 = jnp.float32

    def micro(totals, pair):
        tokens_in, grad_in = pair
        full = (
            lax.all_gather(shards[0], "fsdp", axis=0, tiled=True),
            lax.all_gather(shards[1], "fsdp", axis=0, tiled=True),
            lax.all_gather(shards[2], "fsdp", axis=0, tiled=True),
            lax.all_gather(shards[3], "fsdp", axis=0, tiled=True),
            lax.all_gather(shards[4], "fsdp", axis=0, tiled=True),
            lax.all_gather(shards[5], "fsdp", axis=0, tiled=True),
            lax.all_gather(shards[6], "fsdp", axis=0, tiled=True),
            lax.all_gather(shards[7], "fsdp", axis=0, tiled=True),
            lax.all_gather(shards[8], "fsdp", axis=0, tiled=True),
            lax.all_gather(shards[9], "fsdp", axis=0, tiled=True),
            lax.all_gather(shards[10], "fsdp", axis=0, tiled=True),
            lax.all_gather(shards[11], "fsdp", axis=0, tiled=True),
            lax.all_gather(shards[12], "fsdp", axis=0, tiled=True),
        )
        tokens = tokens_in.astype(f32)
        normal_one, inverse_one = norm_stats(tokens)
        first = (normal_one * full[5] + full[6]).astype(bf16)
        joined = project(first, full[0])
        query = (joined[..., :width] + full[1]).astype(bf16)
        key_own = joined[..., width : 2 * width].astype(bf16)
        value_own = (joined[..., 2 * width :] + full[2]).astype(bf16)
        key_prev, value_prev = from_behind((key_own, value_own), "ctx", 1)
        key_heads = split_heads(jnp.concatenate([key_prev, key_own], axis=1))
        value_heads = split_heads(jnp.concatenate([value_prev, value_own], axis=1))
        query_heads = split_heads(query)
        scores = attention_scores(query_heads, key_heads, allowed, factor)
        top = jnp.max(scores, axis=-1, keepdims=True)
        logsum = top + jnp.log(jnp.sum(jnp.exp(scores - top), axis=-1, keepdims=True))
        probs_low = jnp.exp(scores - logsum).astype(bf16)
        mixed = jnp.einsum("shqk,skhd->sqhd", probs_low, value_heads, preferred_element_type=f32)
        mixed = mixed.reshape(tokens.shape).astype(bf16)
        middle = tokens + project(mixed, full[3]) + full[4]
        normal_two, inverse_two = norm_stats(middle)
        second = (normal_two * full[7] + full[8]).astype(bf16)
        before = project(second, full[9]) + full[10]
        active = jax.nn.gelu(before, approximate=True).astype(bf16)
        result = (middle + project(active, full[11]) + full[12]).astype(bf16)
        again = (
            lax.all_gather(shards[0], "fsdp", axis=0, tiled=True),
            lax.all_gather(shards[1], "fsdp", axis=0, tiled=True),
            lax.all_gather(shards[2], "fsdp", axis=0, tiled=True),
            lax.all_gather(shards[3], "fsdp", axis=0, tiled=True),
            lax.all_gather(shards[4], "fsdp", axis=0, tiled=True),
            lax.all_gather(shards[5], "fsdp", axis=0, tiled=True),
            lax.all_gather(shards[6], "fsdp", axis=0, tiled=True),
            lax.all_gather(shards[7], "fsdp", axis=0, tiled=True),
            lax.all_gather(shards[8], "fsdp", axis=0, tiled=True),
            lax.all_gather(shards[9], "fsdp", axis=0, tiled=True),
            lax.all_gather(shards[10], "fsdp", axis=0, tiled=True),
            lax.all_gather(shards[11], "fsdp", axis=0, tiled=True),
            lax.all_gather(shards[12], "fsdp", axis=0, tiled=True),
        )
        grad_out = grad_in.astype(f32)
        d_down = grad_out.astype(bf16)
        g_wdown = outer_sum(active, d_down)
        g_bdown = column_sum(d_down)
        d_active = project_back(d_down, again[11])
        gelu_back = jax.vjp(partial(jax.nn.gelu, approximate=True), before)[1]
        d_before = gelu_back(d_active)[0].astype(bf16)
        g_wup = outer_sum(second, d_before)
        g_bup = column_sum(d_before)
        d_second = project_back(d_before, again[9])
        g_gmlp = jnp.sum(d_second * normal_two, axis=(0, 1))
        g_smlp = jnp.sum(d_second, axis=(0, 1))
        d_middle = grad_out + norm_back(d_second, normal_two, inverse_two, again[7])
        d_branch = d_middle.astype(bf16)
        g_wmix = outer_sum(mixed, d_branch)
        g_bmix = column_sum(d_branch)
        d_mixed = split_heads(project_back(d_branch, again[3]).astype(bf16))
        scores = attention_scores(query_heads, key_heads, allowed, factor)
        probs = jnp.exp(scores - logsum)
        probs_low = probs.astype(bf16)
        d_probs = jnp.einsum("sqhd,skhd->shqk", d_mixed, value_heads, preferred_element_type=f32)
        d_scores = (
            probs * (d_probs - jnp.sum(d_probs * probs, axis=-1, keepdims=True)) * factor
        ).astype(bf16)
        d_query = jnp.einsum("shqk,skhd->sqhd", d_scores, key_heads, preferred_element_type=f32)
        d_query = d_query.reshape(tokens.shape).astype(bf16)
        d_key_all = jnp.einsum("shqk,sqhd->skhd", d_scores, query_heads, preferred_element_type=f32)
        d_value_all = jnp.einsum("shqk,sqhd->skhd", probs_low, d_mixed, preferred_element_type=f32)
        d_key_all = d_key_all.reshape(tokens.shape[0], 2 * rows, width)
        d_value_all = d_value_all.reshape(tokens.shape[0], 2 * rows, width)
        key_back, value_back = (
            from_behind(d_key_all[:, :rows].astype(jnp.bfloat16), "ctx", -1).astype(jnp.float32),
            from_behind(d_value_all[:, :rows].astype(jnp.bfloat16), "ctx", -1).astype(jnp.float32),
        )
        d_key = (d_key_all[:, rows:] + key_back).astype(bf16)
        d_value = (d_value_all[:, rows:] + value_back).astype(bf16)
        d_joined = jnp.concatenate([d_query, d_key, d_value], axis=-1)
        g_wqkv = outer_sum(first, d_joined)
        g_bquery = column_sum(d_query)
        g_bvalue = column_sum(d_value)
        d_first = project_back(d_joined, again[0])
        g_gattn = jnp.sum(d_first * normal_one, axis=(0, 1))
        g_sattn = jnp.sum(d_first, axis=(0, 1))
        d_tokens = d_middle + norm_back(d_first, normal_one, inverse_one, again[5])
        terms = (
            g_wqkv,
            g_bquery,
            g_bvalue,
            g_wmix,
            g_bmix,
            g_gattn,
            g_sattn,
            g_gmlp,
            g_smlp,
            g_wup,
            g_bup,
            g_wdown,
            g_bdown,
        )
        totals = tuple((left + right for left, right in zip(totals, terms)))
        return (totals, (result, d_tokens))

    totals, (results, grad_tokens) = lax.scan(micro, whole_zeros, (inputs, cotangent))
    shares = jax.tree.map(
        lambda part: part.astype(jnp.float32),
        lax.psum_scatter(for_sending(totals), "fsdp", scatter_dimension=0, tiled=True),
    )
    summed = jax.tree.map(
        lambda part: part.astype(jnp.float32), lax.psum(for_sending(shares), ("rep", "ctx"))
    )
    return (results, grad_tokens) + tuple(summed)


def solution(mesh):
    in_specs = (
        P(None, ("rep", "fsdp"), "ctx", None),
        P("fsdp", None),
        P("fsdp"),
        P("fsdp"),
        P("fsdp", None),
        P("fsdp"),
        P("fsdp"),
        P("fsdp"),
        P("fsdp"),
        P("fsdp"),
        P("fsdp", None),
        P("fsdp"),
        P("fsdp", None),
        P("fsdp"),
        P(None, ("rep", "fsdp"), "ctx", None),
    )
    out_specs = (
        P(None, ("rep", "fsdp"), "ctx", None),
        P(None, ("rep", "fsdp"), "ctx", None),
        P("fsdp", None),
        P("fsdp"),
        P("fsdp"),
        P("fsdp", None),
        P("fsdp"),
        P("fsdp"),
        P("fsdp"),
        P("fsdp"),
        P("fsdp"),
        P("fsdp", None),
        P("fsdp"),
        P("fsdp", None),
        P("fsdp"),
    )
    return jax.shard_map(local, mesh=mesh, in_specs=in_specs, out_specs=out_specs, check_vma=False)
```

profile of v0, /device:TPU:0, one launch (start us, length us, event | category | flops | bytes accessed | tf_op | source)
XLA Modules:
  0.0 1352.4 jit_solution(5778753269937234375)
XLA Ops:
  8.2 974.8 %while.41 = (s32[]{:T(128)}, f32[768,2304]{1,0:T(8,128)}, f32[768]{0:T(1024)}, f32[768]{0:T(1024)}, f32[768,768]{1,0:T(8,128)}, /*index=5*/f32[768]{0:T(1024)}, ...) while((s32[]{:T(128)}, f32[768,2304]{1,0:T(8,128)}, ...), condition=%wide.region_21.22_spmd.clone, body=%wide.region_0.21_spmd.clone.sunk | while | flops 26950144000 | bytes 699213696 | solution.py:228
  19.6 21.4 %all-reduce.30 = (bf16[768]{0:T(1024)(128)(2,1)S(1)}, bf16[768]{0:T(1024)(128)(2,1)S(1)}, bf16[768]{0:T(1024)(128)(2,1)S(1)}, bf16[768]{0:T(1024)(128)(2,1)S(1)}...) all-reduce(bf16[768]{0:T(1024)(128)(2,1)S(1)} %dynamic-update-slice, ...), channel_id=1, replica_groups=mesh['rep'=4,'fsdp'=4,'ctx'=2] {'fsdp'}, use_global_device_ids=true, to_apply=%add.1 | all-reduce | flops 6144 | bytes 24576 | tf_op jit(solution)/shard_map/while
  42.7 41.6 %all-gather.11.cloned.1.call-done = bf16[768,2304]{1,0:T(8,128)(2,1)} async-done(((bf16[192,2304]{1,0:T(8,128)(2,1)}), bf16[768,2304]{1,0:T(8,128)(2,1)}) %all-gather.11.cloned.1.call-update) | async-done | bytes 3538960 | tf_op jit(solution)/shard_map/while/body/eval_jaxpr/all_gather | solution.py:114
  116.7 15.2 %fusion.201 = (f32[12,512]{1,0:T(8,128)S(1)}, f32[12,512,1024]{2,1,0:T(8,128)}) fusion(pred[512,1024]{1,0:T(8,128)(4,1)} %fusion.200, bf16[512,12,64]{0,2,1:T(8,128)(2,1)} %bitcast.212, bf16[1024,12,64]{0,2,1:T(8,128)(2,1)} %bitcast.210), kind=kOutput, calls=%fused_computation.8.clone.1 | convolution fusion | flops 824174592 | bytes 28073984 | tf_op jit(solution)/shard_map/while/body/eval_jaxpr/sqhd,skhd->shqk/dot_general | solution.py:61
  158.9 46.3 %all-gather.13.cloned.1.call-done = bf16[768,3072]{1,0:T(8,128)(2,1)} async-done(((bf16[192,3072]{1,0:T(8,128)(2,1)}), bf16[768,3072]{1,0:T(8,128)(2,1)}) %all-gather.13.cloned.1.call-update) | async-done | bytes 4718608 | tf_op jit(solution)/shard_map/while/body/eval_jaxpr/all_gather | solution.py:123
  212.3 82.2 %all-gather.15.cloned.1.call-done = bf16[3072,768]{1,0:T(8,128)(2,1)} async-done(((bf16[768,768]{1,0:T(8,128)(2,1)}), bf16[3072,768]{1,0:T(8,128)(2,1)}) %all-gather.15.cloned.1.call-update) | async-done | bytes 4718608 | tf_op jit(solution)/shard_map/while/body/eval_jaxpr/all_gather | solution.py:163
  312.2 13.6 %fusion.204 = f32[12,64,1024]{2,1,0:T(8,128)} fusion(bf16[512,12,64]{0,2,1:T(8,128)(2,1)} %bitcast.208, f32[12,512]{1,0:T(8,128)S(1)} %log_add_fusion.2, f32[12,512,1024]{2,1,0:T(8,128)} %get-tuple-element.914, pred[512,1024]{1,0:T(8,128)(4,1)} %fusion.200), kind=kOutput, calls=%fused_computation.107.clone.1 | convolution fusion | flops 830472192 | bytes 29646848 | tf_op jit(solution)/shard_map/while/body/eval_jaxpr/shqk,sqhd->skhd/dot_general | solution.py:193
  335.9 52.3 %convert_reduce_fusion.16 = (f32[12,64]{1,0:T(8,128)S(1)}, bf16[12,64,512]{2,1,0:T(8,128)(2,1)}) fusion(bf16[1024,12,64]{0,2,1:T(8,128)(2,1)} %bitcast.211, f32[12,512,1024]{2,1,0:T(8,128)} %fusion.205, f32[12,512]{1,0:T(8,128)S(1)} %log_add_fusion.2, f32[12,512,1024]{2,1,0:T(8,128)} %get-tuple-element.914, pred[512,1024]{1,0:T(8,128)(4,1)} %fusion.200), kind=kOutput, calls=%fused_computation.77.clone.1 | convolution fusion | flops 875698432 | bytes 53242880 | tf_op jit(solution)/shard_map/while/body/eval_jaxpr/shqk,skhd->sqhd/dot_general | solution.py:190
  388.2 54.3 %fusion.206 = f32[12,64,1024]{2,1,0:T(8,128)} fusion(bf16[512,12,64]{0,2,1:T(8,128)(2,1)} %bitcast.213, f32[12,512,1024]{2,1,0:T(8,128)} %fusion.205, f32[12,512]{1,0:T(8,128)S(1)} %log_add_fusion.2, f32[12,512,1024]{2,1,0:T(8,128)} %get-tuple-element.914, pred[512,1024]{1,0:T(8,128)(4,1)} %fusion.200), kind=kOutput, calls=%fused_computation.10.clone.1 | convolution fusion | flops 874519552 | bytes 54812672 | tf_op jit(solution)/shard_map/while/body/eval_jaxpr/shqk,sqhd->skhd/dot_general | solution.py:192
  502.7 16.6 %all-reduce.30 = (bf16[768]{0:T(1024)(128)(2,1)S(1)}, bf16[768]{0:T(1024)(128)(2,1)S(1)}, bf16[768]{0:T(1024)(128)(2,1)S(1)}, bf16[768]{0:T(1024)(128)(2,1)S(1)}...) all-reduce(bf16[768]{0:T(1024)(128)(2,1)S(1)} %dynamic-update-slice, ...), channel_id=1, replica_groups=mesh['rep'=4,'fsdp'=4,'ctx'=2] {'fsdp'}, use_global_device_ids=true, to_apply=%add.1 | all-reduce | flops 6144 | bytes 24576 | tf_op jit(solution)/shard_map/while
  521.0 43.7 %all-gather.11.cloned.1.call-done = bf16[768,2304]{1,0:T(8,128)(2,1)} async-done(((bf16[192,2304]{1,0:T(8,128)(2,1)}), bf16[768,2304]{1,0:T(8,128)(2,1)}) %all-gather.11.cloned.1.call-update) | async-done | bytes 3538960 | tf_op jit(solution)/shard_map/while/body/eval_jaxpr/all_gather | solution.py:114
  575.1 13.2 all-gather.3
  596.9 15.3 %fusion.201 = (f32[12,512]{1,0:T(8,128)S(1)}, f32[12,512,1024]{2,1,0:T(8,128)}) fusion(pred[512,1024]{1,0:T(8,128)(4,1)} %fusion.200, bf16[512,12,64]{0,2,1:T(8,128)(2,1)} %bitcast.212, bf16[1024,12,64]{0,2,1:T(8,128)(2,1)} %bitcast.210), kind=kOutput, calls=%fused_computation.8.clone.1 | convolution fusion | flops 824174592 | bytes 28073984 | tf_op jit(solution)/shard_map/while/body/eval_jaxpr/sqhd,skhd->shqk/dot_general | solution.py:61
  639.1 46.4 %all-gather.13.cloned.1.call-done = bf16[768,3072]{1,0:T(8,128)(2,1)} async-done(((bf16[192,3072]{1,0:T(8,128)(2,1)}), bf16[768,3072]{1,0:T(8,128)(2,1)}) %all-gather.13.cloned.1.call-update) | async-done | bytes 4718608 | tf_op jit(solution)/shard_map/while/body/eval_jaxpr/all_gather | solution.py:123
  692.7 82.4 %all-gather.15.cloned.1.call-done = bf16[3072,768]{1,0:T(8,128)(2,1)} async-done(((bf16[768,768]{1,0:T(8,128)(2,1)}), bf16[3072,768]{1,0:T(8,128)(2,1)}) %all-gather.15.cloned.1.call-update) | async-done | bytes 4718608 | tf_op jit(solution)/shard_map/while/body/eval_jaxpr/all_gather | solution.py:163
  793.1 13.6 %fusion.204 = f32[12,64,1024]{2,1,0:T(8,128)} fusion(bf16[512,12,64]{0,2,1:T(8,128)(2,1)} %bitcast.208, f32[12,512]{1,0:T(8,128)S(1)} %log_add_fusion.2, f32[12,512,1024]{2,1,0:T(8,128)} %get-tuple-element.914, pred[512,1024]{1,0:T(8,128)(4,1)} %fusion.200), kind=kOutput, calls=%fused_computation.107.clone.1 | convolution fusion | flops 830472192 | bytes 29646848 | tf_op jit(solution)/shard_map/while/body/eval_jaxpr/shqk,sqhd->skhd/dot_general | solution.py:193
  816.8 52.3 %convert_reduce_fusion.16 = (f32[12,64]{1,0:T(8,128)S(1)}, bf16[12,64,512]{2,1,0:T(8,128)(2,1)}) fusion(bf16[1024,12,64]{0,2,1:T(8,128)(2,1)} %bitcast.211, f32[12,512,1024]{2,1,0:T(8,128)} %fusion.205, f32[12,512]{1,0:T(8,128)S(1)} %log_add_fusion.2, f32[12,512,1024]{2,1,0:T(8,128)} %get-tuple-element.914, pred[512,1024]{1,0:T(8,128)(4,1)} %fusion.200), kind=kOutput, calls=%fused_computation.77.clone.1 | convolution fusion | flops 875698432 | bytes 53242880 | tf_op jit(solution)/shard_map/while/body/eval_jaxpr/shqk,skhd->sqhd/dot_general | solution.py:190
  869.1 54.1 %fusion.206 = f32[12,64,1024]{2,1,0:T(8,128)} fusion(bf16[512,12,64]{0,2,1:T(8,128)(2,1)} %bitcast.213, f32[12,512,1024]{2,1,0:T(8,128)} %fusion.205, f32[12,512]{1,0:T(8,128)S(1)} %log_add_fusion.2, f32[12,512,1024]{2,1,0:T(8,128)} %get-tuple-element.914, pred[512,1024]{1,0:T(8,128)(4,1)} %fusion.200), kind=kOutput, calls=%fused_computation.10.clone.1 | convolution fusion | flops 874519552 | bytes 54812672 | tf_op jit(solution)/shard_map/while/body/eval_jaxpr/shqk,sqhd->skhd/dot_general | solution.py:192
  923.2 13.2 select_add_fusion.31
  1015.7 67.2 %reduce-scatter.5.cloned.1.call-done = bf16[192,2304]{1,0:T(8,128)(2,1)} async-done(((bf16[768,2304]{1,0:T(8,128)(2,1)}), bf16[192,2304]{1,0:T(8,128)(2,1)}) %reduce-scatter.5.cloned.1.call-update) | async-done | bytes 884752 | tf_op jit(solution)/shard_map/reduce_scatter | solution.py:231
  1082.9 87.5 %reduce-scatter.9.cloned.1.call-done = bf16[192,3072]{1,0:T(8,128)(2,1)} async-done(((bf16[768,3072]{1,0:T(8,128)(2,1)}), bf16[192,3072]{1,0:T(8,128)(2,1)}) %reduce-scatter.9.cloned.1.call-update) | async-done | bytes 1179664 | tf_op jit(solution)/shard_map/reduce_scatter | solution.py:231
  1170.4 88.0 %reduce-scatter.11.cloned.1.call-done = bf16[768,768]{1,0:T(8,128)(2,1)} async-done(((bf16[3072,768]{1,0:T(8,128)(2,1)}), bf16[768,768]{1,0:T(8,128)(2,1)}) %reduce-scatter.11.cloned.1.call-update) | async-done | bytes 1179664 | tf_op jit(solution)/shard_map/reduce_scatter | solution.py:231
  1260.5 18.3 %all-reduce.28 = (bf16[768]{0:T(1024)(128)(2,1)S(1)}, bf16[768]{0:T(1024)(128)(2,1)S(1)}, bf16[768]{0:T(1024)(128)(2,1)S(1)}, bf16[768]{0:T(1024)(128)(2,1)S(1)}...) all-reduce(bf16[768]{0:T(1024)(128)(2,1)S(1)} %convert_element_type, ...), channel_id=3, replica_groups=mesh['rep'=4,'fsdp'=4,'ctx'=2] {'fsdp'}, use_global_device_ids=true, to_apply=%region_24.25.clone | all-reduce | flops 9216 | bytes 36864
  1296.9 40.1 %all-reduce.33.cloned.1.call-done = (bf16[192,2304]{1,0:T(8,128)(2,1)}, bf16[192,768]{1,0:T(8,128)(2,1)}, bf16[192,3072]{1,0:T(8,128)(2,1)}, bf16[768,768]{1,0:T(8,128)(2,1)}) async-done(((bf16[192,2304]{1,0:T(8,128)(2,1)}, bf16[192,768]{1,0:T(8,128)(2,1)}, bf16[192,3072]{1,0:T(8,128)(2,1)}, bf16[768,768]{1,0:T(8,128)(2,1)}), (bf16[192,2304]{1,0:T(8,128)(2,1)}, bf16[192,768]{1,0:T(8,128)(2,1)}, ...) | async-done | bytes 3538960 | tf_op jit(solution)/shard_map/psum | solution.py:234
  (433 shorter events, 349.3 us)
Async XLA Ops:
  8.7 75.6 %all-gather.11.cloned.1.call-start = ((), (), s32[]{:S(2)}) async-start(), calls=%async_computation.10 | async-start | bytes 4423680 | tf_op jit(solution)/shard_map/while/body/eval_jaxpr/all_gather | solution.py:114
  9.4 146.5 %all-gather.9.cloned.1.call-start = ((), (), s32[]{:S(2)}) async-start(), calls=%async_computation.9 | async-start | bytes 1474560 | tf_op jit(solution)/shard_map/while/body/eval_jaxpr/all_gather | solution.py:117
  10.2 195.0 %all-gather.13.cloned.1.call-start = ((), (), s32[]{:S(2)}) async-start(), calls=%async_computation.11 | async-start | bytes 5898240 | tf_op jit(solution)/shard_map/while/body/eval_jaxpr/all_gather | solution.py:123
  10.9 283.6 %all-gather.15.cloned.1.call-start = ((), (), s32[]{:S(2)}) async-start(), calls=%async_computation.12 | async-start | bytes 5898240 | tf_op jit(solution)/shard_map/while/body/eval_jaxpr/all_gather | solution.py:163
  88.8 21.7 %collective-permute-start = (bf16[1,512,768]{2,1,0:T(8,128)(2,1)S(1)}, bf16[1,512,768]{2,1,0:T(8,128)(2,1)}, u32[]{:S(2)}, u32[]{:S(2)}) collective-permute-start(bf16[1,512,768]{2,1,0:T(8,128)(2,1)S(1)} %get-tuple-element.911), channel_id=1, source_target_pairs={{0,1},{2,3},{4,5},{6,7},{8,9},{10,11},{12,13},{14,15},{16,17},{18,... | collective-permute-start | bytes 2359304 | tf_op jit(solution)/shard_map/while/body/eval_jaxpr/ppermute | solution.py:14
  92.5 20.6 %collective-permute-start.1 = (bf16[1,512,768]{2,1,0:T(8,128)(2,1)}, bf16[1,512,768]{2,1,0:T(8,128)(2,1)}, u32[]{:S(2)}, u32[]{:S(2)}) collective-permute-start(bf16[1,512,768]{2,1,0:T(8,128)(2,1)} %slice.85), channel_id=1, source_target_pairs={{0,1},{2,3},{4,5},{6,7},{8,9},{10,11},{12,13},{14,15},{16,17},{18,... | collective-permute-start | bytes 2359304 | tf_op jit(solution)/shard_map/while/body/eval_jaxpr/ppermute | solution.py:14
  455.4 20.5 %collective-permute-start.2 = (bf16[1,512,768]{1,2,0:T(8,128)(2,1)}, bf16[1,512,768]{1,2,0:T(8,128)(2,1)}, u32[]{:S(2)}, u32[]{:S(2)}) collective-permute-start(bf16[1,512,768]{1,2,0:T(8,128)(2,1)} %slice.86), channel_id=1, source_target_pairs={{1,0},{3,2},{5,4},{7,6},{9,8},{11,10},{13,12},{15,14},{17,16},{19,... | collective-permute-start | bytes 2359304 | tf_op jit(solution)/shard_map/while/body/eval_jaxpr/ppermute | solution.py:14
  463.9 14.9 %collective-permute-start.3 = (bf16[1,512,768]{1,2,0:T(8,128)(2,1)S(1)}, bf16[1,512,768]{1,2,0:T(8,128)(2,1)S(1)}, u32[]{:S(2)}, u32[]{:S(2)}) collective-permute-start(bf16[1,512,768]{1,2,0:T(8,128)(2,1)S(1)} %slice.87), channel_id=1, source_target_pairs={{1,0},{3,2},{5,4},{7,6},{9,8},{11,10},{13,12},{15,14},{17,16},{19,... | collective-permute-start | bytes 2359304 | tf_op jit(solution)/shard_map/while/body/eval_jaxpr/ppermute | solution.py:14
  492.1 72.5 %all-gather.11.cloned.1.call-start = ((), (), s32[]{:S(2)}) async-start(), calls=%async_computation.10 | async-start | bytes 4423680 | tf_op jit(solution)/shard_map/while/body/eval_jaxpr/all_gather | solution.py:114
  492.7 143.5 %all-gather.9.cloned.1.call-start = ((), (), s32[]{:S(2)}) async-start(), calls=%async_computation.9 | async-start | bytes 1474560 | tf_op jit(solution)/shard_map/while/body/eval_jaxpr/all_gather | solution.py:117
  493.2 192.3 %all-gather.13.cloned.1.call-start = ((), (), s32[]{:S(2)}) async-start(), calls=%async_computation.11 | async-start | bytes 5898240 | tf_op jit(solution)/shard_map/while/body/eval_jaxpr/all_gather | solution.py:123
  494.0 281.0 %all-gather.15.cloned.1.call-start = ((), (), s32[]{:S(2)}) async-start(), calls=%async_computation.12 | async-start | bytes 5898240 | tf_op jit(solution)/shard_map/while/body/eval_jaxpr/all_gather | solution.py:163
  569.1 21.8 %collective-permute-start = (bf16[1,512,768]{2,1,0:T(8,128)(2,1)S(1)}, bf16[1,512,768]{2,1,0:T(8,128)(2,1)}, u32[]{:S(2)}, u32[]{:S(2)}) collective-permute-start(bf16[1,512,768]{2,1,0:T(8,128)(2,1)S(1)} %get-tuple-element.911), channel_id=1, source_target_pairs={{0,1},{2,3},{4,5},{6,7},{8,9},{10,11},{12,13},{14,15},{16,17},{18,... | collective-permute-start | bytes 2359304 | tf_op jit(solution)/shard_map/while/body/eval_jaxpr/ppermute | solution.py:14
  572.9 20.3 %collective-permute-start.1 = (bf16[1,512,768]{2,1,0:T(8,128)(2,1)}, bf16[1,512,768]{2,1,0:T(8,128)(2,1)}, u32[]{:S(2)}, u32[]{:S(2)}) collective-permute-start(bf16[1,512,768]{2,1,0:T(8,128)(2,1)} %slice.85), channel_id=1, source_target_pairs={{0,1},{2,3},{4,5},{6,7},{8,9},{10,11},{12,13},{14,15},{16,17},{18,... | collective-permute-start | bytes 2359304 | tf_op jit(solution)/shard_map/while/body/eval_jaxpr/ppermute | solution.py:14
  938.8 22.8 %collective-permute-start.2 = (bf16[1,512,768]{1,2,0:T(8,128)(2,1)}, bf16[1,512,768]{1,2,0:T(8,128)(2,1)}, u32[]{:S(2)}, u32[]{:S(2)}) collective-permute-start(bf16[1,512,768]{1,2,0:T(8,128)(2,1)} %slice.86), channel_id=1, source_target_pairs={{1,0},{3,2},{5,4},{7,6},{9,8},{11,10},{13,12},{15,14},{17,16},{19,... | collective-permute-start | bytes 2359304 | tf_op jit(solution)/shard_map/while/body/eval_jaxpr/ppermute | solution.py:14
  949.6 15.0 %collective-permute-start.3 = (bf16[1,512,768]{1,2,0:T(8,128)(2,1)S(1)}, bf16[1,512,768]{1,2,0:T(8,128)(2,1)S(1)}, u32[]{:S(2)}, u32[]{:S(2)}) collective-permute-start(bf16[1,512,768]{1,2,0:T(8,128)(2,1)S(1)} %slice.87), channel_id=1, source_target_pairs={{1,0},{3,2},{5,4},{7,6},{9,8},{11,10},{13,12},{15,14},{17,16},{19,... | collective-permute-start | bytes 2359304 | tf_op jit(solution)/shard_map/while/body/eval_jaxpr/ppermute | solution.py:14
  983.0 32.7 %reduce-scatter.7.cloned.1.call-start = ((), (), s32[]{:S(2)}) async-start(), calls=%async_computation.5 | async-start | bytes 1474560 | tf_op jit(solution)/shard_map/reduce_scatter | solution.py:231
  985.9 97.0 %reduce-scatter.5.cloned.1.call-start = ((), (), s32[]{:S(2)}) async-start(), calls=%async_computation.4 | async-start | bytes 4423680 | tf_op jit(solution)/shard_map/reduce_scatter | solution.py:231
  991.1 179.3 %reduce-scatter.9.cloned.1.call-start = ((), (), s32[]{:S(2)}) async-start(), calls=%async_computation.6 | async-start | bytes 5898240 | tf_op jit(solution)/shard_map/reduce_scatter | solution.py:231
  998.0 260.5 %reduce-scatter.11.cloned.1.call-start = ((), (), s32[]{:S(2)}) async-start(), calls=%async_computation.7 | async-start | bytes 5898240 | tf_op jit(solution)/shard_map/reduce_scatter | solution.py:231
  1004.4 256.0 %copy-start.30 = (f32[768]{0:T(1024)S(1)}, f32[768]{0:T(1024)}, u32[]{:S(2)}) copy-start(f32[768]{0:T(1024)} %get-tuple-element.425) | copy-start | bytes 9220
  1004.4 256.1 %copy-start.27 = (f32[768]{0:T(1024)S(1)}, f32[768]{0:T(1024)}, u32[]{:S(2)}) copy-start(f32[768]{0:T(1024)} %get-tuple-element.426) | copy-start | bytes 9220
  1004.4 256.1 %copy-start.20 = (f32[3072]{0:T(1024)S(1)}, f32[3072]{0:T(1024)}, u32[]{:S(2)}) copy-start(f32[3072]{0:T(1024)} %get-tuple-element.430) | copy-start | bytes 36868
  1004.5 332.5 %all-reduce.33.cloned.1.call-start = ((), (), s32[]{:S(2)}) async-start(), calls=%async_computation.8 | async-start | bytes 7077888 | tf_op jit(solution)/shard_map/psum | solution.py:234
  (88 other events, 2203.1 us)
Sparse Core Ops, SparseCore 0:
  11.1 73.1 all-gather.10
  85.9 29.1 all-gather.8
  116.6 88.5 all-gather.12
  206.6 87.8 all-gather.14
  494.2 70.3 all-gather.10
  566.0 29.3 all-gather.8
  597.0 88.5 all-gather.12
  687.1 87.8 all-gather.14
Sparse Core Ops, SparseCore 1:
  986.4 29.2 reduce-scatter.6
  1017.9 65.0 reduce-scatter.4
  1085.1 85.3 reduce-scatter.8
  1172.8 85.6 reduce-scatter.10
  1262.2 74.7 all-reduce.32
where the time goes:
time: 1360 us; the launch traced here: 1350 us
  waiting for transfers between devices  640 us (47%)
  matrix products  452 us (33%)
  blocking collectives  94.9 us (7%)
  other arithmetic  79.7 us (6%)
  local copies, waits for them, and re-layouts  45.7 us (3%)
  between operations  17.5 us (1%)
  starting transfers between devices  15.6 us (1%)
    reduce_scatter x4, waiting for transfers between devices, local(): lax.psum_scatter(for_sending(totals), 'fsdp', scatter_dimension=0, tiled=...  254 us
    all_gather x2, waiting for transfers between devices, micro(): lax.all_gather(shards[11], 'fsdp', axis=0, tiled=True)  165 us
    dot_general x2, matrix products, micro(): jnp.einsum('shqk,sqhd->skhd', d_scores, query_heads, preferred_element_ty...  108 us
    dot_general x2, matrix products, micro(): jnp.einsum('shqk,skhd->sqhd', d_scores, key_heads, preferred_element_type...  105 us
    all_gather x2, waiting for transfers between devices, micro(): lax.all_gather(shards[9], 'fsdp', axis=0, tiled=True)  92.7 us
    all_gather x2, waiting for transfers between devices, micro(): lax.all_gather(shards[0], 'fsdp', axis=0, tiled=True)  85.2 us
    dot_general x8, matrix products, outer_sum(): jnp.einsum('sri,srj->ij', left, right, preferred_element_type=jnp.float32)  56.7 us
    dot_general x8, matrix products, project(): jnp.einsum('sri,ij->srj', left, weight, preferred_element_type=jnp.float32)  46.1 us
  transfers between devices with their start and end apart: 21, of which 11 were waited for; matrix products, arithmetic and copies ran while one was open for 16% of the time, Pallas kernels for 0%

commit v1 on v0

--- a/solution.py
+++ b/solution.py
@@ -6,6 +6,27 @@
 
 H = 12
 EPS = 1e-05
+
+
+def ring_gather(x, axis, dim):
+    devices, index, rows = (lax.axis_size(axis), lax.axis_index(axis), x.shape[dim])
+    forward = [(i, (i + 1) % devices) for i in range(devices)]
+    downward = [(i, (i - 1) % devices) for i in range(devices)]
+    filled = jnp.zeros((*x.shape[:dim], devices * rows, *x.shape[dim + 1 :]), x.dtype)
+    filled = lax.dynamic_update_slice_in_dim(filled, x, index * rows, axis=dim)
+    from_left = from_right = x
+    halfway = devices // 2
+    for step in range(1, halfway + 1):
+        from_left = lax.ppermute(from_left, axis, forward)
+        filled = lax.dynamic_update_slice_in_dim(
+            filled, from_left, (index - step) % devices * rows, axis=dim
+        )
+        if step < devices - halfway:
+            from_right = lax.ppermute(from_right, axis, downward)
+            filled = lax.dynamic_update_slice_in_dim(
+                filled, from_right, (index + step) % devices * rows, axis=dim
+            )
+    return filled
 
 
 def from_behind(x, axis, by):
@@ -160,7 +181,7 @@
             lax.all_gather(shards[8], "fsdp", axis=0, tiled=True),
             lax.all_gather(shards[9], "fsdp", axis=0, tiled=True),
             lax.all_gather(shards[10], "fsdp", axis=0, tiled=True),
-            lax.all_gather(shards[11], "fsdp", axis=0, tiled=True),
+            ring_gather(shards[11], "fsdp", 0),
             lax.all_gather(shards[12], "fsdp", axis=0, tiled=True),
         )
         grad_out = grad_in.astype(f32)

time: 1360 us -> 1270 us (0.934)
  waiting for transfers between devices: 640 us -> 541 us
  local copies, waits for them, and re-layouts: 45.7 us -> 65.3 us
    all_gather x2, waiting for transfers between devices: 165 us -> 0.01 us  [micro(): lax.all_gather(shards[11], 'fsdp', axis=0, tiled=True)]
    ppermute x0 -> x3, waiting for transfers between devices: none -> 76.7 us  [the longest x2 52.8 us: ring_gather(): from_left = lax.ppermute(from_left, axis, forward)]
    all_gather x2, waiting for transfers between devices: 92.7 us -> 72.9 us  [micro(): lax.all_gather(shards[9], 'fsdp', axis=0, tiled=True)]
    dynamic_update_slice x0 -> x8, local copies, waits for them, and re-layouts: none -> 16.7 us  [the longest x4 9.73 us: ring_gather(): lax.dynamic_update_slice_in_dim(filled, from_left, (index - step) % devic...]
  transfers between devices with their start and end apart: 21 -> 24, of which waited for: 11 -> 12; matrix products, arithmetic and copies ran while one was open for 16% -> 43% of each run, Pallas kernels for 0% -> 0%
where the time goes in v1:
time: 1270 us
  waiting for transfers between devices  541 us (43%)
  matrix products  448 us (35%)
  blocking collectives  90.5 us (7%)
  other arithmetic  80.2 us (6%)
  local copies, waits for them, and re-layouts  65.3 us (5%)
  starting transfers between devices  20.5 us (2%)
  between operations  17.5 us (1%)
    reduce_scatter x4, waiting for transfers between devices, local(): lax.psum_scatter(for_sending(totals), 'fsdp', scatter_dimension=0, tiled=...  254 us
    dot_general x2, matrix products, micro(): jnp.einsum('shqk,sqhd->skhd', d_scores, query_heads, preferred_element_ty...  108 us
    dot_general x2, matrix products, micro(): jnp.einsum('shqk,skhd->sqhd', d_scores, key_heads, preferred_element_type...  105 us
    all_gather x2, waiting for transfers between devices, micro(): lax.all_gather(shards[0], 'fsdp', axis=0, tiled=True)  91.2 us
    all_gather x2, waiting for transfers between devices, micro(): lax.all_gather(shards[9], 'fsdp', axis=0, tiled=True)  72.9 us
    dot_general x8, matrix products, outer_sum(): jnp.einsum('sri,srj->ij', left, right, preferred_element_type=jnp.float32)  59.6 us
    ppermute x2, waiting for transfers between devices, ring_gather(): from_left = lax.ppermute(from_left, axis, forward)  52.8 us
    dot_general x8, matrix products, project(): jnp.einsum('sri,ij->srj', left, weight, preferred_element_type=jnp.float32)  41.5 us
  transfers between devices with their start and end apart: 24, of which 12 were waited for; matrix products, arithmetic and copies ran while one was open for 43% of the time, Pallas kernels for 0%

profile of v1, /device:TPU:0, one launch (start us, length us, event | category | flops | bytes accessed | tf_op | source)
XLA Modules:
  0.0 1268.6 jit_solution(4901477788543122277)
XLA Ops:
  13.2 27.1 %collective-permute-done.4 = bf16[768,768]{1,0:T(8,128)(2,1)} collective-permute-done((bf16[768,768]{1,0:T(8,128)(2,1)}, bf16[768,768]{1,0:T(8,128)(2,1)}, u32[]{:S(2)}, u32[]{:S(2)}) %collective-permute-start.4) | collective-permute-done | bytes 1179680 | tf_op jit(solution)/shard_map/while/body/eval_jaxpr/ppermute | solution.py:20
  40.4 23.9 %collective-permute-done.5 = bf16[768,768]{1,0:T(8,128)(2,1)} collective-permute-done((bf16[768,768]{1,0:T(8,128)(2,1)}, bf16[768,768]{1,0:T(8,128)(2,1)}, u32[]{:S(2)}, u32[]{:S(2)}) %collective-permute-start.5) | collective-permute-done | bytes 1179680 | tf_op jit(solution)/shard_map/while/body/eval_jaxpr/ppermute | solution.py:25
  64.3 25.7 %collective-permute-done.6 = bf16[768,768]{1,0:T(8,128)(2,1)} collective-permute-done((bf16[768,768]{1,0:T(8,128)(2,1)}, bf16[768,768]{1,0:T(8,128)(2,1)}, u32[]{:S(2)}, u32[]{:S(2)}) %collective-permute-start.6) | collective-permute-done | bytes 1179680 | tf_op jit(solution)/shard_map/while/body/eval_jaxpr/ppermute | solution.py:20
  90.0 808.5 %while.41 = (s32[]{:T(128)}, f32[768,2304]{1,0:T(8,128)}, f32[768]{0:T(1024)}, f32[768]{0:T(1024)}, f32[768,768]{1,0:T(8,128)}, /*index=5*/f32[768]{0:T(1024)}, ...) while((s32[]{:T(128)}, f32[768,2304]{1,0:T(8,128)}, ...), condition=%wide.region_21.22_spmd.clone, body=%wide.region_0.21_spmd.clone.sunk | while | flops 26950144000 | bytes 763714880 | solution.py:249
  96.7 17.7 %all-reduce.30 = (bf16[768]{0:T(1024)(128)(2,1)S(1)}, bf16[768]{0:T(1024)(128)(2,1)S(1)}, bf16[768]{0:T(1024)(128)(2,1)S(1)}, bf16[768]{0:T(1024)(128)(2,1)S(1)}...) all-reduce(bf16[768]{0:T(1024)(128)(2,1)S(1)} %dynamic-update-slice, ...), channel_id=1, replica_groups=mesh['rep'=4,'fsdp'=4,'ctx'=2] {'fsdp'}, use_global_device_ids=true, to_apply=%add.1 | all-reduce | flops 6144 | bytes 24576 | tf_op jit(solution)/shard_map/while
  117.9 44.2 %all-gather.11.cloned.1.call-done = bf16[768,2304]{1,0:T(8,128)(2,1)} async-done(((bf16[192,2304]{1,0:T(8,128)(2,1)}), bf16[768,2304]{1,0:T(8,128)(2,1)}) %all-gather.11.cloned.1.call-update) | async-done | bytes 3538960 | tf_op jit(solution)/shard_map/while/body/eval_jaxpr/all_gather | solution.py:135
  180.9 13.1 %all-gather.3 = bf16[4,1,768]{2,1,0:T(2,128)(2,1)S(1)} all-gather(bf16[1,1,768]{2,1,0:T(2,128)(2,1)S(1)} %reshape.647), channel_id=1, replica_groups=mesh['rep'=4,'fsdp'=4,'ctx'=2] {'fsdp'}, dimensions={0}, use_global_device_ids=true | all-gather | bytes 7680 | tf_op jit(solution)/shard_map/while/body/eval_jaxpr/all_gather | solution.py:145
  205.2 14.5 %fusion.201 = (f32[12,512]{1,0:T(8,128)S(1)}, f32[12,512,1024]{2,1,0:T(8,128)}) fusion(pred[512,1024]{1,0:T(8,128)(4,1)} %fusion.200, bf16[512,12,64]{0,2,1:T(8,128)(2,1)} %bitcast.212, bf16[1024,12,64]{0,2,1:T(8,128)(2,1)} %bitcast.210), kind=kOutput, calls=%fused_computation.8.clone.1 | convolution fusion | flops 824174592 | bytes 28073984 | tf_op jit(solution)/shard_map/while/body/eval_jaxpr/sqhd,skhd->shqk/dot_general | solution.py:82
  246.6 36.4 %all-gather.13.cloned.1.call-done = bf16[768,3072]{1,0:T(8,128)(2,1)} async-done(((bf16[192,3072]{1,0:T(8,128)(2,1)}), bf16[768,3072]{1,0:T(8,128)(2,1)}) %all-gather.13.cloned.1.call-update) | async-done | bytes 4718608 | tf_op jit(solution)/shard_map/while/body/eval_jaxpr/all_gather | solution.py:144
  333.2 52.3 %convert_reduce_fusion.16 = (f32[12,64]{1,0:T(8,128)S(1)}, bf16[12,64,512]{2,1,0:T(8,128)(2,1)}) fusion(bf16[1024,12,64]{0,2,1:T(8,128)(2,1)} %bitcast.211, f32[12,512,1024]{2,1,0:T(8,128)} %fusion.205, f32[12,512]{1,0:T(8,128)S(1)} %log_add_fusion.2, f32[12,512,1024]{2,1,0:T(8,128)} %get-tuple-element.967, pred[512,1024]{1,0:T(8,128)(4,1)} %fusion.200), kind=kOutput, calls=%fused_computation.77.clone.1 | convolution fusion | flops 875698432 | bytes 53242880 | tf_op jit(solution)/shard_map/while/body/eval_jaxpr/shqk,skhd->sqhd/dot_general | solution.py:211
  385.6 54.1 %fusion.206 = f32[12,64,1024]{2,1,0:T(8,128)} fusion(bf16[512,12,64]{0,2,1:T(8,128)(2,1)} %bitcast.213, f32[12,512,1024]{2,1,0:T(8,128)} %fusion.205, f32[12,512]{1,0:T(8,128)S(1)} %log_add_fusion.2, f32[12,512,1024]{2,1,0:T(8,128)} %get-tuple-element.967, pred[512,1024]{1,0:T(8,128)(4,1)} %fusion.200), kind=kOutput, calls=%fused_computation.10.clone.1 | convolution fusion | flops 874519552 | bytes 54812672 | tf_op jit(solution)/shard_map/while/body/eval_jaxpr/shqk,sqhd->skhd/dot_general | solution.py:213
  495.7 16.1 %all-reduce.30 = (bf16[768]{0:T(1024)(128)(2,1)S(1)}, bf16[768]{0:T(1024)(128)(2,1)S(1)}, bf16[768]{0:T(1024)(128)(2,1)S(1)}, bf16[768]{0:T(1024)(128)(2,1)S(1)}...) all-reduce(bf16[768]{0:T(1024)(128)(2,1)S(1)} %dynamic-update-slice, ...), channel_id=1, replica_groups=mesh['rep'=4,'fsdp'=4,'ctx'=2] {'fsdp'}, use_global_device_ids=true, to_apply=%add.1 | all-reduce | flops 6144 | bytes 24576 | tf_op jit(solution)/shard_map/while
  515.3 47.0 %all-gather.11.cloned.1.call-done = bf16[768,2304]{1,0:T(8,128)(2,1)} async-done(((bf16[192,2304]{1,0:T(8,128)(2,1)}), bf16[768,2304]{1,0:T(8,128)(2,1)}) %all-gather.11.cloned.1.call-update) | async-done | bytes 3538960 | tf_op jit(solution)/shard_map/while/body/eval_jaxpr/all_gather | solution.py:135
  581.2 13.1 %all-gather.3 = bf16[4,1,768]{2,1,0:T(2,128)(2,1)S(1)} all-gather(bf16[1,1,768]{2,1,0:T(2,128)(2,1)S(1)} %reshape.647), channel_id=1, replica_groups=mesh['rep'=4,'fsdp'=4,'ctx'=2] {'fsdp'}, dimensions={0}, use_global_device_ids=true | all-gather | bytes 7680 | tf_op jit(solution)/shard_map/while/body/eval_jaxpr/all_gather | solution.py:145
  605.4 14.5 %fusion.201 = (f32[12,512]{1,0:T(8,128)S(1)}, f32[12,512,1024]{2,1,0:T(8,128)}) fusion(pred[512,1024]{1,0:T(8,128)(4,1)} %fusion.200, bf16[512,12,64]{0,2,1:T(8,128)(2,1)} %bitcast.212, bf16[1024,12,64]{0,2,1:T(8,128)(2,1)} %bitcast.210), kind=kOutput, calls=%fused_computation.8.clone.1 | convolution fusion | flops 824174592 | bytes 28073984 | tf_op jit(solution)/shard_map/while/body/eval_jaxpr/sqhd,skhd->shqk/dot_general | solution.py:82
  646.8 36.4 %all-gather.13.cloned.1.call-done = bf16[768,3072]{1,0:T(8,128)(2,1)} async-done(((bf16[192,3072]{1,0:T(8,128)(2,1)}), bf16[768,3072]{1,0:T(8,128)(2,1)}) %all-gather.13.cloned.1.call-update) | async-done | bytes 4718608 | tf_op jit(solution)/shard_map/while/body/eval_jaxpr/all_gather | solution.py:144
  733.3 52.3 %convert_reduce_fusion.16 = (f32[12,64]{1,0:T(8,128)S(1)}, bf16[12,64,512]{2,1,0:T(8,128)(2,1)}) fusion(bf16[1024,12,64]{0,2,1:T(8,128)(2,1)} %bitcast.211, f32[12,512,1024]{2,1,0:T(8,128)} %fusion.205, f32[12,512]{1,0:T(8,128)S(1)} %log_add_fusion.2, f32[12,512,1024]{2,1,0:T(8,128)} %get-tuple-element.967, pred[512,1024]{1,0:T(8,128)(4,1)} %fusion.200), kind=kOutput, calls=%fused_computation.77.clone.1 | convolution fusion | flops 875698432 | bytes 53242880 | tf_op jit(solution)/shard_map/while/body/eval_jaxpr/shqk,skhd->sqhd/dot_general | solution.py:211
  785.7 54.1 %fusion.206 = f32[12,64,1024]{2,1,0:T(8,128)} fusion(bf16[512,12,64]{0,2,1:T(8,128)(2,1)} %bitcast.213, f32[12,512,1024]{2,1,0:T(8,128)} %fusion.205, f32[12,512]{1,0:T(8,128)S(1)} %log_add_fusion.2, f32[12,512,1024]{2,1,0:T(8,128)} %get-tuple-element.967, pred[512,1024]{1,0:T(8,128)(4,1)} %fusion.200), kind=kOutput, calls=%fused_computation.10.clone.1 | convolution fusion | flops 874519552 | bytes 54812672 | tf_op jit(solution)/shard_map/while/body/eval_jaxpr/shqk,sqhd->skhd/dot_general | solution.py:213
  852.6 12.9 %select_add_fusion.31 = f32[3072,768]{1,0:T(8,128)} fusion(f32[3072,768]{1,0:T(8,128)} %get-tuple-element.1061, pred[]{:T(512)S(6)} %compare.6, bf16[2,1,512,768]{3,2,1,0:T(8,128)(2,1)S(1)} %copy-done.17, s32[]{:T(128)S(6)} %copy.84, f32[512,3072]{1,0:T(8,128)} %copy-done.61, f32[3072]{0:T(1024)S(1)} %bitcast.221), kind=kOutput, calls=%fused_computation.12.clone.1 | convolution fusion | flops 2436366336 | bytes 25964548 | tf_op jit(solution)/shard_map/while/body/eval_jaxpr/sri,srj->ij/dot_general | solution.py:66
  931.8 67.2 %reduce-scatter.5.cloned.1.call-done = bf16[192,2304]{1,0:T(8,128)(2,1)} async-done(((bf16[768,2304]{1,0:T(8,128)(2,1)}), bf16[192,2304]{1,0:T(8,128)(2,1)}) %reduce-scatter.5.cloned.1.call-update) | async-done | bytes 884752 | tf_op jit(solution)/shard_map/reduce_scatter | solution.py:252
  999.0 87.5 %reduce-scatter.9.cloned.1.call-done = bf16[192,3072]{1,0:T(8,128)(2,1)} async-done(((bf16[768,3072]{1,0:T(8,128)(2,1)}), bf16[192,3072]{1,0:T(8,128)(2,1)}) %reduce-scatter.9.cloned.1.call-update) | async-done | bytes 1179664 | tf_op jit(solution)/shard_map/reduce_scatter | solution.py:252
  1086.5 88.0 %reduce-scatter.11.cloned.1.call-done = bf16[768,768]{1,0:T(8,128)(2,1)} async-done(((bf16[3072,768]{1,0:T(8,128)(2,1)}), bf16[768,768]{1,0:T(8,128)(2,1)}) %reduce-scatter.11.cloned.1.call-update) | async-done | bytes 1179664 | tf_op jit(solution)/shard_map/reduce_scatter | solution.py:252
  1176.7 18.3 %all-reduce.28 = (bf16[768]{0:T(1024)(128)(2,1)S(1)}, bf16[768]{0:T(1024)(128)(2,1)S(1)}, bf16[768]{0:T(1024)(128)(2,1)S(1)}, bf16[768]{0:T(1024)(128)(2,1)S(1)}...) all-reduce(bf16[768]{0:T(1024)(128)(2,1)S(1)} %convert_element_type, ...), channel_id=3, replica_groups=mesh['rep'=4,'fsdp'=4,'ctx'=2] {'fsdp'}, use_global_device_ids=true, to_apply=%region_24.25.clone | all-reduce | flops 9216 | bytes 36864
  1212.9 40.2 %all-reduce.33.cloned.1.call-done = (bf16[192,2304]{1,0:T(8,128)(2,1)}, bf16[192,768]{1,0:T(8,128)(2,1)}, bf16[192,3072]{1,0:T(8,128)(2,1)}, bf16[768,768]{1,0:T(8,128)(2,1)}) async-done(((bf16[192,2304]{1,0:T(8,128)(2,1)}, bf16[192,768]{1,0:T(8,128)(2,1)}, bf16[192,3072]{1,0:T(8,128)(2,1)}, bf16[768,768]{1,0:T(8,128)(2,1)}), (bf16[192,2304]{1,0:T(8,128)(2,1)}, bf16[192,768]{1,0:T(8,128)(2,1)}, ...) | async-done | bytes 3538960 | tf_op jit(solution)/shard_map/psum | solution.py:255
  (507 shorter events, 387.8 us)
Async XLA Ops:
  8.0 32.3 %collective-permute-start.4 = (bf16[768,768]{1,0:T(8,128)(2,1)}, bf16[768,768]{1,0:T(8,128)(2,1)}, u32[]{:S(2)}, u32[]{:S(2)}) collective-permute-start(bf16[768,768]{1,0:T(8,128)(2,1)} %param.29), channel_id=1, source_target_pairs={{0,2},{2,4},{4,6},{6,0},{1,3},{3,5},{5,7},{7,1},{8,10},{10,12},{12... | collective-permute-start | bytes 3538952 | tf_op jit(solution)/shard_map/while/body/eval_jaxpr/ppermute | solution.py:20
  11.1 53.2 %collective-permute-start.5 = (bf16[768,768]{1,0:T(8,128)(2,1)}, bf16[768,768]{1,0:T(8,128)(2,1)}, u32[]{:S(2)}, u32[]{:S(2)}) collective-permute-start(bf16[768,768]{1,0:T(8,128)(2,1)} %param.29), channel_id=1, source_target_pairs={{0,6},{2,0},{4,2},{6,4},{1,7},{3,1},{5,3},{7,5},{8,14},{10,8},{12,... | collective-permute-start | bytes 3538952 | tf_op jit(solution)/shard_map/while/body/eval_jaxpr/ppermute | solution.py:25
  40.3 49.7 %collective-permute-start.6 = (bf16[768,768]{1,0:T(8,128)(2,1)}, bf16[768,768]{1,0:T(8,128)(2,1)}, u32[]{:S(2)}, u32[]{:S(2)}) collective-permute-start(bf16[768,768]{1,0:T(8,128)(2,1)} %collective-permute-done.4), channel_id=1, source_target_pairs={{0,2},{2,4},{4,6},{6,0},{1,3},{3,5},{5,7},{7,1},{8,10},{10,12},{12... | collective-permute-start | bytes 3538952 | tf_op jit(solution)/shard_map/while/body/eval_jaxpr/ppermute | solution.py:20
  90.1 72.0 %all-gather.11.cloned.1.call-start = ((), (), s32[]{:S(2)}) async-start(), calls=%async_computation.10 | async-start | bytes 4423680 | tf_op jit(solution)/shard_map/while/body/eval_jaxpr/all_gather | solution.py:135
  90.9 152.8 %all-gather.9.cloned.1.call-start = ((), (), s32[]{:S(2)}) async-start(), calls=%async_computation.9 | async-start | bytes 1474560 | tf_op jit(solution)/shard_map/while/body/eval_jaxpr/all_gather | solution.py:138
  91.6 191.4 %all-gather.13.cloned.1.call-start = ((), (), s32[]{:S(2)}) async-start(), calls=%async_computation.11 | async-start | bytes 5898240 | tf_op jit(solution)/shard_map/while/body/eval_jaxpr/all_gather | solution.py:144
  92.3 368.8 %all-gather.15.cloned.1.call-start = ((), (), s32[]{:S(2)}) async-start(), calls=%async_computation.12 | async-start | bytes 5898240 | tf_op jit(solution)/shard_map/while/body/eval_jaxpr/all_gather | solution.py:146
  168.8 30.2 %collective-permute-start = (bf16[1,512,768]{2,1,0:T(8,128)(2,1)S(1)}, bf16[1,512,768]{2,1,0:T(8,128)(2,1)}, u32[]{:S(2)}, u32[]{:S(2)}) collective-permute-start(bf16[1,512,768]{2,1,0:T(8,128)(2,1)S(1)} %get-tuple-element.964), channel_id=1, source_target_pairs={{0,1},{2,3},{4,5},{6,7},{8,9},{10,11},{12,13},{14,15},{16,17},{18,... | collective-permute-start | bytes 2359304 | tf_op jit(solution)/shard_map/while/body/eval_jaxpr/ppermute | solution.py:35
  176.3 25.1 %collective-permute-start.1 = (bf16[1,512,768]{2,1,0:T(8,128)(2,1)}, bf16[1,512,768]{2,1,0:T(8,128)(2,1)}, u32[]{:S(2)}, u32[]{:S(2)}) collective-permute-start(bf16[1,512,768]{2,1,0:T(8,128)(2,1)} %slice.85), channel_id=1, source_target_pairs={{0,1},{2,3},{4,5},{6,7},{8,9},{10,11},{12,13},{14,15},{16,17},{18,... | collective-permute-start | bytes 2359304 | tf_op jit(solution)/shard_map/while/body/eval_jaxpr/ppermute | solution.py:35
  321.6 150.2 %collective-permute-start.2 = (bf16[1,512,768]{1,2,0:T(8,128)(2,1)}, bf16[1,512,768]{1,2,0:T(8,128)(2,1)}, u32[]{:S(2)}, u32[]{:S(2)}) collective-permute-start(bf16[1,512,768]{1,2,0:T(8,128)(2,1)} %slice.86), channel_id=1, source_target_pairs={{1,0},{3,2},{5,4},{7,6},{9,8},{11,10},{13,12},{15,14},{17,16},{19,... | collective-permute-start | bytes 2359304 | tf_op jit(solution)/shard_map/while/body/eval_jaxpr/ppermute | solution.py:35
  442.1 32.7 %collective-permute-start.3 = (bf16[1,512,768]{1,2,0:T(8,128)(2,1)}, bf16[1,512,768]{1,2,0:T(8,128)(2,1)}, u32[]{:S(2)}, u32[]{:S(2)}) collective-permute-start(bf16[1,512,768]{1,2,0:T(8,128)(2,1)} %slice.87), channel_id=1, source_target_pairs={{1,0},{3,2},{5,4},{7,6},{9,8},{11,10},{13,12},{15,14},{17,16},{19,... | collective-permute-start | bytes 2359304 | tf_op jit(solution)/shard_map/while/body/eval_jaxpr/ppermute | solution.py:35
  489.3 73.1 %all-gather.11.cloned.1.call-start = ((), (), s32[]{:S(2)}) async-start(), calls=%async_computation.10 | async-start | bytes 4423680 | tf_op jit(solution)/shard_map/while/body/eval_jaxpr/all_gather | solution.py:135
  489.8 154.0 %all-gather.9.cloned.1.call-start = ((), (), s32[]{:S(2)}) async-start(), calls=%async_computation.9 | async-start | bytes 1474560 | tf_op jit(solution)/shard_map/while/body/eval_jaxpr/all_gather | solution.py:138
  490.4 192.8 %all-gather.13.cloned.1.call-start = ((), (), s32[]{:S(2)}) async-start(), calls=%async_computation.11 | async-start | bytes 5898240 | tf_op jit(solution)/shard_map/while/body/eval_jaxpr/all_gather | solution.py:144
  491.2 374.3 %all-gather.15.cloned.1.call-start = ((), (), s32[]{:S(2)}) async-start(), calls=%async_computation.12 | async-start | bytes 5898240 | tf_op jit(solution)/shard_map/while/body/eval_jaxpr/all_gather | solution.py:146
  569.1 30.2 %collective-permute-start = (bf16[1,512,768]{2,1,0:T(8,128)(2,1)S(1)}, bf16[1,512,768]{2,1,0:T(8,128)(2,1)}, u32[]{:S(2)}, u32[]{:S(2)}) collective-permute-start(bf16[1,512,768]{2,1,0:T(8,128)(2,1)S(1)} %get-tuple-element.964), channel_id=1, source_target_pairs={{0,1},{2,3},{4,5},{6,7},{8,9},{10,11},{12,13},{14,15},{16,17},{18,... | collective-permute-start | bytes 2359304 | tf_op jit(solution)/shard_map/while/body/eval_jaxpr/ppermute | solution.py:35
  576.6 25.0 %collective-permute-start.1 = (bf16[1,512,768]{2,1,0:T(8,128)(2,1)}, bf16[1,512,768]{2,1,0:T(8,128)(2,1)}, u32[]{:S(2)}, u32[]{:S(2)}) collective-permute-start(bf16[1,512,768]{2,1,0:T(8,128)(2,1)} %slice.85), channel_id=1, source_target_pairs={{0,1},{2,3},{4,5},{6,7},{8,9},{10,11},{12,13},{14,15},{16,17},{18,... | collective-permute-start | bytes 2359304 | tf_op jit(solution)/shard_map/while/body/eval_jaxpr/ppermute | solution.py:35
  721.7 154.4 %collective-permute-start.2 = (bf16[1,512,768]{1,2,0:T(8,128)(2,1)}, bf16[1,512,768]{1,2,0:T(8,128)(2,1)}, u32[]{:S(2)}, u32[]{:S(2)}) collective-permute-start(bf16[1,512,768]{1,2,0:T(8,128)(2,1)} %slice.86), channel_id=1, source_target_pairs={{1,0},{3,2},{5,4},{7,6},{9,8},{11,10},{13,12},{15,14},{17,16},{19,... | collective-permute-start | bytes 2359304 | tf_op jit(solution)/shard_map/while/body/eval_jaxpr/ppermute | solution.py:35
  842.2 36.8 %collective-permute-start.3 = (bf16[1,512,768]{1,2,0:T(8,128)(2,1)}, bf16[1,512,768]{1,2,0:T(8,128)(2,1)}, u32[]{:S(2)}, u32[]{:S(2)}) collective-permute-start(bf16[1,512,768]{1,2,0:T(8,128)(2,1)} %slice.87), channel_id=1, source_target_pairs={{1,0},{3,2},{5,4},{7,6},{9,8},{11,10},{13,12},{15,14},{17,16},{19,... | collective-permute-start | bytes 2359304 | tf_op jit(solution)/shard_map/while/body/eval_jaxpr/ppermute | solution.py:35
  898.5 33.3 %reduce-scatter.7.cloned.1.call-start = ((), (), s32[]{:S(2)}) async-start(), calls=%async_computation.5 | async-start | bytes 1474560 | tf_op jit(solution)/shard_map/reduce_scatter | solution.py:252
  901.4 97.6 %reduce-scatter.5.cloned.1.call-start = ((), (), s32[]{:S(2)}) async-start(), calls=%async_computation.4 | async-start | bytes 4423680 | tf_op jit(solution)/shard_map/reduce_scatter | solution.py:252
  906.7 179.8 %reduce-scatter.9.cloned.1.call-start = ((), (), s32[]{:S(2)}) async-start(), calls=%async_computation.6 | async-start | bytes 5898240 | tf_op jit(solution)/shard_map/reduce_scatter | solution.py:252
  913.6 261.0 %reduce-scatter.11.cloned.1.call-start = ((), (), s32[]{:S(2)}) async-start(), calls=%async_computation.7 | async-start | bytes 5898240 | tf_op jit(solution)/shard_map/reduce_scatter | solution.py:252
  920.0 333.0 %all-reduce.33.cloned.1.call-start = ((), (), s32[]{:S(2)}) async-start(), calls=%async_computation.8 | async-start | bytes 7077888 | tf_op jit(solution)/shard_map/psum | solution.py:255
  (119 other events, 2966.7 us)
Sparse Core Ops, SparseCore 0:
  92.5 69.4 all-gather.10
  163.6 29.2 all-gather.8
  194.5 88.5 all-gather.12
  284.5 87.8 all-gather.14
  491.4 70.9 all-gather.10
  563.8 29.2 all-gather.8
  594.7 88.5 all-gather.12
  684.8 87.8 all-gather.14
Sparse Core Ops, SparseCore 1:
  901.9 29.9 reduce-scatter.6
  934.0 64.9 reduce-scatter.4
  1001.2 85.3 reduce-scatter.8
  1088.9 85.6 reduce-scatter.10
  1178.3 74.7 all-reduce.32
